TPU v7x, 256 devices: a whole 4x4x8 slice. The times are simulated.
256 devices in a mesh: dp: 64 (over z_lo, y, x, core), ckpt: 4 (over z_hi).
Axes of the slice: x: 4, y: 4, z: 8 (z_hi: 4, z_lo: 2; z = z_hi * 2 + z_lo), core: 2. Of those that a mesh axis runs over, the one named last changes fastest.
Arguments:
- layer_input: bfloat16 [32768, 6144], P(('dp', 'ckpt')), may hold values from -6 to 6
- out_grad: bfloat16 [32768, 6144], P(('dp', 'ckpt')), may hold values from -6 to 6
- router_weight: bfloat16 [32768], P(('dp', 'ckpt')), may hold values from 0.049804688 to 1
- token_slot: int32 [32768], P(('dp', 'ckpt')), may hold values from -1 to 7, as said below
- slot_token: int32 [2048], P(('dp', 'ckpt')), may hold values from -1 to 127, as said below
- gate_weight: bfloat16 [6144, 8192], P('ckpt', 'dp'), may hold values from -0.078125 to 0.078125
- up_weight: bfloat16 [6144, 8192], P('ckpt', 'dp'), may hold values from -0.078125 to 0.078125
- down_weight: bfloat16 [6144, 8192], P('ckpt', 'dp'), may hold values from -0.078125 to 0.078125
Outputs:
- input_grad: bfloat16 [32768, 6144], P(('dp', 'ckpt'))
- router_grad: float32 [32768], P(('dp', 'ckpt'))
- gate_grad: float32 [6144, 8192], P('ckpt', 'dp')
- up_grad: float32 [6144, 8192], P('ckpt', 'dp')
- down_grad: float32 [6144, 8192], P('ckpt', 'dp')
Inputs may be any that keep to these rules, and one draw needn't show every extreme that they name: `token_slot`: for each token, its row among the rows that its device sends to the expert, or -1 if the router did not send it there. A device's live rows are 0 to n - 1 for some n of 1 to 8. For each of a device's 8 rows, the index among that device's tokens of the token in it, or -1 for an empty row. Live rows come first; token_slot and slot_token are inverse to each other. In every draw all devices of some group along ckpt fill all 8 rows.
All inputs are finite; a program needn't handle non-finite values.
Results may differ from a plain program's by a relative error of at most 0.0049.
Values may be sent and summed in bfloat16 or wider, within the bound.
A program may use at most 128 MiB of HBM per device.

v0:
```python
import jax
import jax.numpy as jnp
from jax import lax
from jax.sharding import PartitionSpec as P


def local(
    layer_input,
    out_grad,
    router_weight,
    token_slot,
    slot_token,
    gate_weight,
    up_weight,
    down_weight,
):
    members = lax.axis_size("ckpt")
    row_count = slot_token.shape[0]
    is_live = slot_token >= 0
    safe_index = jnp.maximum(slot_token, 0)
    rows_input = jnp.where(
        is_live[:, None], jnp.take(layer_input, safe_index, axis=0), jnp.zeros((), jnp.bfloat16)
    )
    rows_grad = jnp.where(
        is_live[:, None], jnp.take(out_grad, safe_index, axis=0), jnp.zeros((), jnp.bfloat16)
    )
    rows_router = jnp.where(
        is_live, jnp.take(router_weight, safe_index, axis=0), jnp.zeros((), jnp.bfloat16)
    )
    router_tile = jnp.broadcast_to(rows_router[:, None], (row_count, members))
    quarter_input, quarter_grad, quarter_router = (
        lax.all_to_all(rows_input, "ckpt", split_axis=1, concat_axis=0, tiled=True),
        lax.all_to_all(rows_grad, "ckpt", split_axis=1, concat_axis=0, tiled=True),
        lax.all_to_all(router_tile, "ckpt", split_axis=1, concat_axis=0, tiled=True),
    )
    all_input, all_grad, all_router = (
        lax.all_gather(quarter_input, "dp", axis=0, tiled=True),
        lax.all_gather(quarter_grad, "dp", axis=0, tiled=True),
        lax.all_gather(quarter_router, "dp", axis=0, tiled=True),
    )
    gate_part = jnp.dot(all_input, gate_weight, preferred_element_type=jnp.float32)
    up_part = jnp.dot(all_input, up_weight, preferred_element_type=jnp.float32)
    back_part = jnp.dot(all_grad, down_weight, preferred_element_type=jnp.float32)
    gate_pre, up_pre, act_grad = lax.psum((gate_part, up_part, back_part), "ckpt")
    sigmoid_g = jax.nn.sigmoid(gate_pre)
    active = sigmoid_g * gate_pre * up_pre
    router_f = all_router.astype(jnp.float32)
    scaled = (router_f * active).astype(jnp.bfloat16)
    router_part = jnp.sum(active * act_grad, axis=1)
    act_delta = router_f * act_grad
    gate_delta = (act_delta * up_pre * sigmoid_g * (1.0 + gate_pre * (1.0 - sigmoid_g))).astype(
        jnp.bfloat16
    )
    up_delta = (act_delta * sigmoid_g * gate_pre).astype(jnp.bfloat16)
    input_part = jnp.einsum(
        "rh,dh->rd", gate_delta, gate_weight, preferred_element_type=jnp.float32
    )
    input_part = input_part + jnp.einsum(
        "rh,dh->rd", up_delta, up_weight, preferred_element_type=jnp.float32
    )
    input_sums, router_sums = (
        lax.psum_scatter(input_part, "dp", scatter_dimension=0, tiled=True),
        lax.psum_scatter(router_part, "dp", scatter_dimension=0, tiled=True),
    )
    input_quarters = input_sums.astype(jnp.bfloat16)
    input_rows = lax.all_to_all(input_quarters, "ckpt", split_axis=0, concat_axis=1, tiled=True)
    own_router = lax.dynamic_slice_in_dim(
        router_sums, lax.axis_index("ckpt") * row_count, row_count, 0
    )
    has_row = token_slot >= 0
    token_index = jnp.maximum(token_slot, 0)
    input_grad = jnp.where(
        has_row[:, None], jnp.take(input_rows, token_index, axis=0), jnp.zeros((), jnp.bfloat16)
    )
    router_grad = jnp.where(
        has_row, jnp.take(own_router, token_index, axis=0), jnp.zeros((), jnp.float32)
    )
    gate_grad = jnp.einsum("rd,rh->dh", all_input, gate_delta, preferred_element_type=jnp.float32)
    up_grad = jnp.einsum("rd,rh->dh", all_input, up_delta, preferred_element_type=jnp.float32)
    down_grad = jnp.einsum("rd,rh->dh", all_grad, scaled, preferred_element_type=jnp.float32)
    return (input_grad, router_grad, gate_grad, up_grad, down_grad)


def solution(mesh):
    return jax.shard_map(
        local,
        mesh=mesh,
        in_specs=(
            P(("dp", "ckpt"), None),
            P(("dp", "ckpt"), None),
            P(("dp", "ckpt")),
            P(("dp", "ckpt")),
            P(("dp", "ckpt")),
            P("ckpt", "dp"),
            P("ckpt", "dp"),
            P("ckpt", "dp"),
        ),
        out_specs=(
            P(("dp", "ckpt"), None),
            P(("dp", "ckpt")),
            P("ckpt", "dp"),
            P("ckpt", "dp"),
            P("ckpt", "dp"),
        ),
        check_vma=False,
    )
```

profile of v0, /device:TPU:2, one launch (start us, length us, event | category | flops | bytes accessed | tf_op | source)
XLA Modules:
  0.0 759.6 jit_solution(3806657502283674632)
XLA Ops:
  7.2 0.0 copy-start
  7.2 0.0 all-gather.5.cloned.1.call-start
  7.2 0.8 broadcast_maximum_fusion
  8.0 0.7 broadcast_compare_fusion.1
  8.7 0.0 copy-done
  8.7 0.0 copy-start.4
  8.7 0.6 gather_fusion.3
  9.3 2.3 gather_fusion.2
  11.6 0.1 select_select_fusion.2
  11.7 17.0 %all_to_all.73 = bf16[8,4,1536]{2,0,1:T(8,128)(2,1)} all-to-all(bf16[8,4,1536]{2,0,1:T(8,128)(2,1)S(1)} %bitcast.46), channel_id=1, replica_groups=mesh['dp'=64,'ckpt'=4] {'ckpt'}, dimensions={1} | all-to-all | bytes 196608 | tf_op jit(solution)/shard_map/all_to_all | solution.py:32
  28.7 0.0 all-gather.5.cloned.1.call-update
  28.7 0.0 all-gather.3.cloned.1.call-start
  28.8 11.3 %all_to_all.74 = bf16[8,4,1536]{2,0,1:T(8,128)(2,1)} all-to-all(bf16[8,4,1536]{2,0,1:T(8,128)(2,1)S(1)} %bitcast.45), channel_id=1, replica_groups=mesh['dp'=64,'ckpt'=4] {'ckpt'}, dimensions={1} | all-to-all | bytes 196608 | tf_op jit(solution)/shard_map/all_to_all | solution.py:33
  40.0 0.0 all-gather.3.cloned.1.call-update
  40.0 0.0 all-reduce.5.cloned.1.call-start
  40.1 95.2 %all-gather.5.cloned.1.call-done = bf16[2048,1536]{1,0:T(8,128)(2,1)} async-done(((bf16[32,1536]{1,0:T(8,128)(2,1)}), bf16[2048,1536]{1,0:T(8,128)(2,1)}) %all-gather.5.cloned.1.call-update) | async-done | bytes 6291472 | tf_op jit(solution)/shard_map/all_gather | solution.py:37
  135.3 5.7 fusion.8
  141.1 0.0 copy-done.4
  141.1 0.0 copy-done.2
  141.1 2.9 fusion.7
  143.9 0.0 copy-start.1
  143.9 0.0 copy-start.10
  143.9 0.0 copy-start.8
  143.9 102.3 %all-gather.3.cloned.1.call-done = bf16[2048,1536]{1,0:T(8,128)(2,1)} async-done(((bf16[32,1536]{1,0:T(8,128)(2,1)}), bf16[2048,1536]{1,0:T(8,128)(2,1)}) %all-gather.3.cloned.1.call-update) | async-done | bytes 6291472 | tf_op jit(solution)/shard_map/all_gather | solution.py:38
  246.2 0.0 copy-done.7
  246.2 5.6 fusion.6
  251.8 0.0 copy-start.3
  251.8 0.0 all-reduce.5.cloned.1.call-update
  251.8 0.0 copy-done.1
  251.8 0.6 gather_fusion
  252.5 0.0 copy-done.10
  252.5 0.6 broadcast_in_dim.80
  253.1 6.4 all-to-all-start
  259.5 0.0 reduce-scatter.2.cloned.1.call-start
  259.5 0.0 copy-done.8
  259.5 0.6 fusion.4
  260.8 6.5 all-to-all-done
  267.3 0.1 reshape.97
  267.4 0.2 dynamic-update-slice
  267.6 149.4 %all-reduce = bf16[2048]{0:T(1024)(128)(2,1)S(1)} all-reduce(bf16[2048]{0:T(1024)(128)(2,1)S(1)} %dynamic-update-slice), channel_id=1, replica_groups=mesh['dp'=64,'ckpt'=4] {'dp'}, use_global_device_ids=true, to_apply=%add | all-reduce | flops 2048 | bytes 8192
  417.0 0.0 all-reduce.5.cloned.1.call-done
  417.0 2.7 multiply_reduce_fusion
  419.7 0.0 copy-done.3
  419.7 1.8 fusion.9
  421.5 6.4 convolution_add_fusion
  427.9 0.0 reduce-scatter.2.cloned.1.call-update
  428.6 0.0 copy-done.9
  428.7 141.1 %all-reduce.1 = f32[2048]{0:T(1024)S(1)} all-reduce(f32[2048]{0:T(1024)S(1)} %get-tuple-element.9), channel_id=3, replica_groups=mesh['dp'=64,'ckpt'=4] {'dp'}, use_global_device_ids=true, to_apply=%region_5.7.clone | all-reduce | flops 2048 | bytes 16384
  569.8 0.1 dynamic_slice.3
  569.8 0.7 fusion.5
  570.5 5.7 fusion.10
  576.2 5.7 fusion.11
  581.9 0.0 slice-done
  581.9 0.0 copy-done.5
  581.9 0.0 copy-done.6
  581.9 0.0 slice-done.1
  581.9 3.1 fusion
  585.0 149.0 %reduce-scatter.2.cloned.1.call-done = f32[32,1536]{1,0:T(8,128)} async-done(((f32[2048,1536]{1,0:T(8,128)}), f32[32,1536]{1,0:T(8,128)}) %reduce-scatter.2.cloned.1.call-update) | async-done | bytes 196624 | tf_op jit(solution)/shard_map/reduce_scatter | solution.py:62
  734.0 1.6 convert_bitcast_fusion
  735.6 6.1 all-to-all-start.3
  741.7 5.6 fusion.3
  747.3 2.9 all-to-all-done.3
  750.2 1.5 gather_fusion.1
  751.7 1.4 select_select_fusion
  (16 shorter events, 0.1 us)
Async XLA Ops:
  7.2 1.5 copy-start
  7.2 128.2 %all-gather.5.cloned.1.call-start = ((), (), s32[]{:S(2)}) async-start(), calls=%async_computation.6 | async-start | bytes 6389760 | tf_op jit(solution)/shard_map/all_gather | solution.py:37
  8.7 132.4 %copy-start.4 = (bf16[1536,128]{1,0:T(8,128)(2,1)S(1)}, bf16[1536,128]{1,0:T(8,128)(2,1)}, u32[]{:S(2)}) copy-start(bf16[1536,128]{1,0:T(8,128)(2,1)} %param.16) | copy-start | bytes 1179652
  28.7 217.5 %all-gather.3.cloned.1.call-start = ((), (), s32[]{:S(2)}) async-start(), calls=%async_computation.5 | async-start | bytes 6389760 | tf_op jit(solution)/shard_map/all_gather | solution.py:38
  40.0 376.9 %all-reduce.5.cloned.1.call-start = ((), (), s32[]{:S(2)}) async-start(), calls=%async_computation.8 | async-start | bytes 6291456 | tf_op jit(solution)/shard_map/psum | solution.py:44
  135.3 5.7 copy-start.2
  141.1 105.2 %copy-start.7 = (bf16[1536,128]{1,0:T(8,128)(2,1)S(1)}, bf16[1536,128]{1,0:T(8,128)(2,1)}, u32[]{:S(2)}) copy-start(bf16[1536,128]{1,0:T(8,128)(2,1)} %param.17) | copy-start | bytes 1179652
  143.9 107.9 %copy-start.1 = (bf16[128]{0:T(256)(128)(2,1)S(1)}, bf16[128]{0:T(256)(128)(2,1)}, u32[]{:S(2)}) copy-start(bf16[128]{0:T(256)(128)(2,1)} %param.12) | copy-start | bytes 772
  143.9 108.5 %copy-start.10 = (s32[8]{0:T(128)S(1)}, s32[8]{0:T(128)}, u32[]{:S(2)}) copy-start(s32[8]{0:T(128)} %param.14) | copy-start | bytes 100
  143.9 115.6 %copy-start.8 = (u32[256]{0:T(256)S(1)}, u32[256]{0:T(256)}, u32[]{:S(2)}) copy-start(u32[256]{0:T(256)} %constant.88) | copy-start | bytes 3076
  251.8 167.9 %copy-start.3 = (bf16[1536,128]{1,0:T(8,128)(2,1)S(1)}, bf16[1536,128]{1,0:T(8,128)(2,1)}, u32[]{:S(2)}) copy-start(bf16[1536,128]{1,0:T(8,128)(2,1)} %param.15) | copy-start | bytes 1179652
  253.1 14.2 %all-to-all-start = ((bf16[8,4,1]{0,2,1:T(2,128)(2,1)}), bf16[8,4,1]{0,2,1:T(2,128)(2,1)S(1)}, u32[]{:S(2)}, u32[]{:S(2)}) async-start(bf16[8,4,1]{0,2,1:T(2,128)(2,1)} %broadcast_in_dim.80), calls=%async_computation | async-start | bytes 4096 | tf_op jit(solution)/shard_map/all_to_all | solution.py:34
  259.5 474.5 %reduce-scatter.2.cloned.1.call-start = ((), (), s32[]{:S(2)}) async-start(), calls=%async_computation.7 | async-start | bytes 12779520 | tf_op jit(solution)/shard_map/reduce_scatter | solution.py:62
  427.9 0.7 copy-start.9
  570.5 11.3 %slice-start = ((s8[6291456]{0:T(1024)(128)(4,1)}), s8[4194304]{0:T(1024)(128)(4,1)S(1)}, s32[]{:S(2)}) async-start(s8[6291456]{0:T(1024)(128)(4,1)} %bitcast.41), calls=%async_computation.9 | async-start | bytes 8388608
  570.5 11.3 %copy-start.5 = (f32[2048,128]{1,0:T(8,128)S(1)}, f32[2048,128]{1,0:T(8,128)}, u32[]{:S(2)}) copy-start(f32[2048,128]{1,0:T(8,128)} %get-tuple-element.6) | copy-start | bytes 3145732
  570.5 11.3 %copy-start.6 = (f32[2048,128]{1,0:T(8,128)S(1)}, f32[2048,128]{1,0:T(8,128)}, u32[]{:S(2)}) copy-start(f32[2048,128]{1,0:T(8,128)} %get-tuple-element.7) | copy-start | bytes 3145732
  576.2 5.7 slice-start.1
  735.6 14.6 %all-to-all-start.3 = ((bf16[4,8,1536]{2,1,0:T(8,128)(2,1)}), bf16[4,8,1536]{2,1,0:T(8,128)(2,1)S(1)}, u32[]{:S(2)}, u32[]{:S(2)}) async-start(bf16[4,8,1536]{2,1,0:T(8,128)(2,1)} %convert_bitcast_fusion), calls=%async_computation.4 | async-start | bytes 196608 | tf_op jit(solution)/shard_map/all_to_all | solution.py:66
Sparse Core Ops, SparseCore 0:
  28.8 106.4 all-gather.4
  137.2 108.9 all-gather.2
  251.9 126.2 all-reduce.4
  428.1 305.8 reduce-scatter.1
where the time goes:
time: 765 us; the launch traced here: 760 us
  waiting for transfers between devices  356 us (47%)
  blocking collectives  319 us (42%)
  matrix products  36.8 us (5%)
  between operations  15.2 us (2%)
  other arithmetic  12.8 us (2%)
  starting transfers between devices  12.7 us (2%)
    unnamed x2, blocking collectives  290 us
    reduce_scatter x1, waiting for transfers between devices, local(): lax.psum_scatter(input_part, 'dp', scatter_dimension=0, tiled=True)  149 us
    all_gather x1, waiting for transfers between devices, local(): lax.all_gather(quarter_grad, 'dp', axis=0, tiled=True)  102 us
    all_gather x1, waiting for transfers between devices, local(): lax.all_gather(quarter_input, 'dp', axis=0, tiled=True)  95.2 us
    all_to_all x1, blocking collectives, local(): lax.all_to_all(rows_input, 'ckpt', split_axis=1, concat_axis=0, tiled=True)  17 us
  transfers between devices with their start and end apart: 6, of which 5 were waited for; matrix products, arithmetic and copies ran while one was open for 4% of the time, Pallas kernels for 0%

commit v1 on v0

v1 whole, which is shorter than its diff:
```python
import functools

import jax
import jax.numpy as jnp
from jax import lax
from jax.experimental import pallas as pl
from jax.experimental.pallas import tpu as pltpu
from jax.sharding import PartitionSpec as P

MESH = pl.DeviceIdType.MESH
BF = jnp.bfloat16
F32 = jnp.float32

RIGHT, LEFT, OPP = 1, 2, 3
OFFSET = (0, 1, 3, 2)
MIRROR = (0, 2, 1, 3)
QUARTER = 1536
EXTRA = 128
WIDE = QUARTER + EXTRA
HID = 128
SLOTS = 8
SHARD = 32
UNITS = 160


def kernel(
    slot_ref,
    router_ref,
    x_hbm,
    g_hbm,
    wg_hbm,
    wu_hbm,
    wd_hbm,
    rows_out,
    router_out,
    own_gate,
    own_up,
    own_down,
    peer_part,
    xbuf,
    gbuf,
    wcat,
    stage_x,
    stage_g,
    land_x,
    land_g,
    xa,
    ga,
    pre_own,
    pre_right,
    pre_left,
    zs,
    zr,
    dl,
    router_part,
    dmat,
    e_own,
    e_right,
    e_left,
    es,
    er,
    f_own,
    f_right,
    f_left,
    fs,
    fr,
    zl_send,
    zl_recv,
    last_send,
    last_recv,
    part_send,
    send_sem,
    recv_sem,
    local_sem,
):
    g = lax.axis_index("dp")
    m = lax.axis_index("ckpt")
    core = lax.rem(g, 2)
    x = lax.rem(g // 2, 4)
    y = lax.rem(g // 8, 4)
    zlo = g // 32

    def device(dx, dy, dz):
        return (zlo_of(dz) * 32 + lax.rem(y + dy, 4) * 8 + lax.rem(x + dx, 4) * 2 + core, m)

    def zlo_of(dz):
        return 1 - zlo if dz else zlo

    a_right = device(core, 1 - core, 0)
    a_left = device(3 * core, 3 * (1 - core), 0)
    b_right = device(1 - core, core, 0)
    b_left = device(3 * (1 - core), 3 * core, 0)
    partner = device(0, 0, 1)
    sibling = (g + 1 - 2 * core, m)
    z_at = [(g, lax.rem(m + OFFSET[p], 4)) for p in range(4)]
    z_right, z_left = z_at[RIGHT], z_at[LEFT]

    sent = []

    def send(src, dst, to):
        unit = len(sent)
        copy = pltpu.make_async_remote_copy(
            src_ref=src,
            dst_ref=dst,
            send_sem=send_sem.at[unit],
            recv_sem=recv_sem.at[unit],
            device_id=to,
            device_id_type=MESH,
        )
        copy.start()
        sent.append(copy)
        return copy

    locals_ = []

    def local(src, dst):
        copy = pltpu.make_async_copy(src, dst, local_sem.at[len(locals_)])
        copy.start()
        locals_.append(copy)
        return copy

    class Gather:
        def __init__(self, at, right, left):
            self.at, self.right, self.left = at, right, left

        def start(self, half):
            at = self.at
            if half == 0:
                self.r0 = send(at(0, 0), at(LEFT, 0), self.right)
                self.l0 = send(at(0, 0), at(RIGHT, 0), self.left)
            else:
                self.l1 = send(at(0, 1), at(RIGHT, 1), self.left)
                self.r1 = send(at(0, 1), at(LEFT, 1), self.right)

        def relay(self):
            at = self.at
            self.r0.wait_recv()
            self.o0 = send(at(LEFT, 0), at(OPP, 0), self.right)
            self.l1.wait_recv()
            self.o1 = send(at(RIGHT, 1), at(OPP, 1), self.left)

        def finish_right(self):
            self.l0.wait_recv()

        def finish_left(self):
            self.r1.wait_recv()

        def finish_opposite(self):
            self.o0.wait_recv()
            self.o1.wait_recv()

        def finish(self):
            self.finish_right()
            self.finish_left()
            self.finish_opposite()

    class Reduce:
        def __init__(self, src, dst, right, left):
            self.src, self.dst, self.right, self.left = src, dst, right, left
            self.units = [None] * 6

        def one(self, unit):
            to = self.right if unit in (0, 2, 4) else self.left
            self.units[unit] = send(self.src(unit), self.dst(unit), to)

        def start(self):
            for unit in (0, 1, 2, 3):
                self.one(unit)

        def relay(self, add):
            self.units[0].wait_recv()
            add(0)
            self.one(4)
            self.units[1].wait_recv()
            add(1)
            self.one(5)

        def finish(self):
            for unit in (2, 3, 4, 5):
                self.units[unit].wait_recv()

    load_x = local(x_hbm, xbuf)
    load_g = local(g_hbm, gbuf)
    weights = (wg_hbm, wu_hbm, wd_hbm)
    load_w = [local(w, wcat.at[j, :, pl.ds(0, HID)]) for j, w in enumerate(weights)]

    barrier = pltpu.get_barrier_semaphore()
    peers = [a_right, a_left, b_right, b_left, partner, sibling] + z_at[1:]
    for peer in peers:
        pl.semaphore_signal(barrier, inc=1, device_id=peer, device_id_type=MESH)

    row = lax.broadcasted_iota(jnp.int32, (16, 128), 0)
    col = lax.broadcasted_iota(jnp.int32, (16, 128), 1)
    pick = jnp.zeros((16, 128), F32)
    for s in range(SLOTS):
        pick = jnp.where((row == s) & (col == slot_ref[s]), 1.0, pick)
    router_rows = jnp.sum(pick[:SLOTS] * router_ref[...].astype(F32), axis=1, keepdims=True)
    router_tile = jnp.broadcast_to(router_rows, (SLOTS, EXTRA)).astype(BF)
    pick = pick.astype(BF)
    quarters = [pl.ds(pl.multiple_of(lax.rem(m + OFFSET[p], 4) * QUARTER, 128), QUARTER) for p in range(4)]

    def rows_of(buf, p):
        got = jnp.dot(pick, buf[:, quarters[p]], preferred_element_type=F32)
        return got[:SLOTS]

    load_x.wait()
    own_x = rows_of(xbuf, 0)
    for p in (1, 2, 3):
        stage_x[p, :, 0:QUARTER] = rows_of(xbuf, p).astype(BF)
        stage_x[p, :, QUARTER:WIDE] = router_tile
    load_g.wait()
    own_g = rows_of(gbuf, 0)
    for p in (1, 2, 3):
        stage_g[p] = rows_of(gbuf, p).astype(BF)
    stage_x[0, :, 0:QUARTER] = own_x.astype(BF)
    stage_x[0, :, QUARTER:WIDE] = router_tile
    stage_g[0] = own_g.astype(BF)

    pl.semaphore_wait(barrier, len(peers))

    first_x = [send(stage_x.at[p], land_x.at[MIRROR[p]], z_at[p]) for p in (3, 1, 2)]
    first_g = [send(stage_g.at[p], land_g.at[MIRROR[p]], z_at[p]) for p in (3, 1, 2)]
    sent_w = [send(w, wcat.at[j, :, pl.ds(HID, HID)], sibling) for j, w in enumerate(weights)]

    def make_shard(stage, land, out):
        parts = [stage[0].astype(F32)] + [land[p].astype(F32) for p in (1, 2, 3)]
        out[0:16] = jnp.concatenate(parts[0:2], axis=0).astype(BF)
        out[16:32] = jnp.concatenate(parts[2:4], axis=0).astype(BF)

    arrays = (xa, ga)
    gather_b = [Gather(lambda p, h, t=t: t.at[p, 0, h], b_right, b_left) for t in arrays]
    gather_a = [
        [Gather(lambda p, h, t=t, k=k: t.at[k, p, h], a_right, a_left) for t in arrays] for k in range(4)
    ]

    pair = []
    for i, (stage, land, first) in enumerate(((stage_x, land_x, first_x), (stage_g, land_g, first_g))):
        for copy in first:
            copy.wait_recv()
        make_shard(stage, land, arrays[i].at[0, 0, 0])
        pair.append(send(arrays[i].at[0, 0, 0], arrays[i].at[0, 0, 1], partner))
        gather_a[0][i].start(0)
        gather_b[i].start(0)
    for i in range(2):
        pair[i].wait_recv()
        gather_a[0][i].start(1)
        gather_b[i].start(1)

    reduce_z = [Reduce(lambda u, k=k: zs.at[k, u], lambda u, k=k: zr.at[k, u], z_right, z_left) for k in range(4)]
    gather_z = [Gather(lambda p, h, k=k: dl.at[k, p, h], z_right, z_left) for k in range(4)]
    reduce_a = [Reduce(lambda u, k=k: es.at[k, u], lambda u, k=k: er.at[k, u], a_right, a_left) for k in range(4)]
    reduce_b = Reduce(lambda u: fs.at[u], lambda u: fr.at[u], b_right, b_left)

    def forward(k):
        lhs_x = xa[k, :, :, :, 0:QUARTER].reshape(256, QUARTER)
        lhs_g = ga[k].reshape(256, QUARTER)
        for j, lhs in enumerate((lhs_x, lhs_x, lhs_g)):
            pre = jnp.dot(lhs, wcat[j], preferred_element_type=F32)
            piece = [
                [
                    jnp.concatenate([pre[(q * 4 + p) * 8 : (q * 4 + p) * 8 + 8] for q in range(4 * h, 4 * h + 4)], axis=0)
                    for h in range(2)
                ]
                for p in range(4)
            ]
            zs[k, 0, j] = piece[OPP][0]
            zs[k, 1, j] = piece[OPP][1]
            zs[k, 2, j] = piece[RIGHT][1]
            zs[k, 3, j] = piece[LEFT][0]
            pre_own[k, 0, j] = piece[0][0]
            pre_own[k, 1, j] = piece[0][1]
            pre_right[k, j] = piece[RIGHT][0]
            pre_left[k, j] = piece[LEFT][1]
        reduce_z[k].start()

    def relay_z(k):
        def add(side):
            mine = pre_left if side else pre_right
            zs[k, 4 + side] = mine[k] + zr[k, side]

        reduce_z[k].relay(add)

    def elementwise(k):
        reduce_z[k].finish()
        for h in range(2):
            near, far = (2, 5) if h else (3, 4)
            total = pre_own[k, h] + zr[k, near] + zr[k, far]
            gate_pre, up_pre, act_grad = total[0], total[1], total[2]
            router = xa[k, 2 * h : 2 * h + 2, :, 0:16, QUARTER:WIDE].astype(F32)[:, :, 0:8].reshape(32, EXTRA)
            router = jnp.concatenate([router, router], axis=1)
            sigmoid_g = jax.nn.sigmoid(gate_pre)
            active = sigmoid_g * gate_pre * up_pre
            dl[k, 0, h, 2] = (router * active).astype(BF)
            act_delta = router * act_grad
            dl[k, 0, h, 0] = (act_delta * up_pre * sigmoid_g * (1.0 + gate_pre * (1.0 - sigmoid_g))).astype(BF)
            dl[k, 0, h, 1] = (act_delta * sigmoid_g * gate_pre).astype(BF)
            product = active * act_grad
            router_part[k, pl.ds(32 * h, 32)] = product[:, 0:128] + product[:, 128:256]
            gather_z[k].start(h)

    def extra_of(v):
        high = v.astype(BF)
        low = (v - high.astype(F32)).astype(BF)
        return jnp.concatenate([high.astype(F32), low.astype(F32), jnp.zeros((16, EXTRA), F32)], axis=0)

    def backward(k):
        for j in range(3):
            d = dl[k, :, :, j].astype(F32)
            parts = []
            for q in range(8):
                for p in range(4):
                    parts.append(d[p, q // 4, (q % 4) * 8 : (q % 4) * 8 + 8])
            dmat[j, pl.ds(256 * k, 256)] = jnp.concatenate(parts, axis=0).astype(BF)

        def block(n, carry):
            cols = pl.ds(pl.multiple_of(n * 256, 256), 256)
            nt = (((1,), (1,)), ((), ()))
            rows = pl.ds(256 * k, 256)
            dx = lax.dot_general(dmat[0, rows], wcat[0, cols, :], nt, preferred_element_type=F32)
            dx = dx + lax.dot_general(dmat[1, rows], wcat[1, cols, :], nt, preferred_element_type=F32)
            unit = [dx[32 * q : 32 * q + 32] for q in range(8)]
            e_own[k, 0, :, cols] = unit[0]
            e_own[k, 1, :, cols] = unit[1]
            e_right[k, :, cols] = unit[2]
            es[k, 2, :, cols] = unit[3].astype(BF)
            es[k, 3, :, cols] = unit[4].astype(BF)
            e_left[k, :, cols] = unit[5]
            es[k, 0, :, cols] = unit[6].astype(BF)
            es[k, 1, :, cols] = unit[7].astype(BF)
            return carry

        lax.fori_loop(0, QUARTER // 256, block, 0)
        tail = slice(QUARTER, WIDE)
        ex = [extra_of(router_part[k, pl.ds(8 * q, 8)]) for q in range(8)]
        e_own[k, 0, :, tail] = ex[0]
        e_own[k, 1, :, tail] = ex[1]
        e_right[k, :, tail] = ex[2]
        es[k, 2, :, tail] = ex[3].astype(BF)
        es[k, 3, :, tail] = ex[4].astype(BF)
        e_left[k, :, tail] = ex[5]
        es[k, 0, :, tail] = ex[6].astype(BF)
        es[k, 1, :, tail] = ex[7].astype(BF)
        reduce_a[k].start()

    def put(ref, total):
        ref[:, 0:QUARTER] = total[:, 0:QUARTER].astype(BF)
        v = total[0:8, QUARTER:WIDE] + total[8:16, QUARTER:WIDE]
        ref[:, QUARTER:WIDE] = extra_of(v).astype(BF)

    def relay_a(k):
        def add(side):
            mine = e_left if side else e_right
            put(es.at[k, 4 + side], mine[k] + er[k, side].astype(F32))

        reduce_a[k].relay(add)

    def finish_a(k):
        reduce_a[k].finish()
        total = [
            e_own[k, h] + er[k, (3, 2)[h]].astype(F32) + er[k, (4, 5)[h]].astype(F32) for h in range(2)
        ]
        if k == 0:
            f_own[0] = total[0]
            f_own[1] = total[1]
        elif k == RIGHT:
            f_right[...] = total[0]
            put(fs.at[2], total[1])
            reduce_b.one(2)
        elif k == LEFT:
            put(fs.at[3], total[0])
            f_left[...] = total[1]
            reduce_b.one(3)
        else:
            put(fs.at[0], total[0])
            reduce_b.one(0)
            put(fs.at[1], total[1])
            reduce_b.one(1)

    def start_a(k):
        for i in range(2):
            if k == RIGHT:
                gather_b[i].finish_right()
            elif k == LEFT:
                gather_b[i].finish_left()
            else:
                gather_b[i].finish_opposite()
            gather_a[k][i].start(0)
            gather_a[k][i].start(1)

    def relay_gather(k):
        for i in range(2):
            gather_a[k][i].relay()

    def finish_gather(k):
        for i in range(2):
            gather_a[k][i].finish()

    part = []

    def weight_block(n, carry):
        cols = pl.ds(pl.multiple_of(n * 256, 256), 256)
        tn = (((0,), (0,)), ((), ()))
        lhs_x = xa[:, :, :, :, cols].reshape(1024, 256)
        lhs_g = ga[:, :, :, :, cols].reshape(1024, 256)
        for j, (lhs, own) in enumerate(((lhs_x, own_gate), (lhs_x, own_up), (lhs_g, own_down))):
            dw = lax.dot_general(lhs, dmat[j], tn, preferred_element_type=F32)
            own[cols, :] = dw[:, 0:HID]
            part_send[j, cols, :] = dw[:, HID:]
        return carry

    def weight_grads():
        lax.fori_loop(0, QUARTER // 256, weight_block, 0)
        for j in range(3):
            part.append(send(part_send.at[j], peer_part.at[j], sibling))

    for i in range(2):
        gather_a[0][i].relay()
        gather_b[i].relay()
    start_a(RIGHT)
    finish_gather(0)
    for copy in load_w:
        copy.wait()
    for copy in sent_w:
        copy.wait_recv()
    forward(0)
    relay_gather(1)
    start_a(LEFT)
    relay_z(0)
    finish_gather(1)
    forward(1)
    elementwise(0)
    relay_gather(2)
    start_a(OPP)
    relay_z(1)
    gather_z[0].relay()
    elementwise(1)
    finish_gather(2)
    forward(2)
    gather_z[0].finish()
    backward(0)
    relay_gather(3)
    relay_z(2)
    gather_z[1].relay()
    relay_a(0)
    elementwise(2)
    finish_gather(3)
    forward(3)
    gather_z[1].finish()
    backward(1)
    relay_z(3)
    gather_z[2].relay()
    relay_a(1)
    finish_a(0)
    elementwise(3)
    gather_z[2].finish()
    backward(2)
    gather_z[3].relay()
    relay_a(2)
    finish_a(1)
    gather_z[3].finish()
    backward(3)
    finish_a(2)
    relay_a(3)
    weight_grads()
    finish_a(3)

    def add_b(side):
        mine = f_left if side else f_right
        put(fs.at[4 + side], mine[...] + fr[side].astype(F32))

    reduce_b.relay(add_b)
    reduce_b.finish()
    for h in (1, 0):
        total = f_own[h] + fr[(3, 2)[h]].astype(F32) + fr[(4, 5)[h]].astype(F32)
        if h:
            put(zl_send, total)
            swap = send(zl_send, zl_recv, partner)
        else:
            f_own[0] = total
    swap.wait_recv()
    total = f_own[0] + zl_recv[...].astype(F32)
    router_sum = total[0:8, QUARTER:WIDE] + total[8:16, QUARTER:WIDE]
    router_out[...] = jnp.broadcast_to(jnp.sum(router_sum, axis=1, keepdims=True), (SLOTS, EXTRA))
    for p in range(4):
        last_send[p] = total[8 * p : 8 * p + 8, 0:QUARTER].astype(BF)
    last = [send(last_send.at[p], last_recv.at[MIRROR[p]], z_at[p]) for p in (3, 1, 2)]
    rows_out[m] = last_send[0]
    for p, copy in zip((3, 1, 2), last):
        copy.wait_recv()
    for p in (1, 2, 3):
        rows_out[lax.rem(m + OFFSET[p], 4)] = last_recv[p]
    for copy in part:
        copy.wait_recv()
    for copy in sent:
        copy.wait_send()


def local_step(
    layer_input,
    out_grad,
    router_weight,
    token_slot,
    slot_token,
    gate_weight,
    up_weight,
    down_weight,
):
    any_ = pl.BlockSpec(memory_space=pl.ANY)
    vmem = pl.BlockSpec(memory_space=pltpu.VMEM)
    grad = jax.ShapeDtypeStruct((QUARTER, HID), F32)
    rows, router, own_gate, own_up, own_down, peer = pl.pallas_call(
        kernel,
        out_shape=(
            jax.ShapeDtypeStruct((4, SLOTS, QUARTER), BF),
            jax.ShapeDtypeStruct((SLOTS, EXTRA), F32),
            grad,
            grad,
            grad,
            jax.ShapeDtypeStruct((3, QUARTER, HID), F32),
        ),
        in_specs=[pl.BlockSpec(memory_space=pltpu.SMEM), vmem, any_, any_, any_, any_, any_],
        out_specs=(vmem, vmem, vmem, vmem, vmem, any_),
        scratch_shapes=[
            pltpu.VMEM((128, 4 * QUARTER), BF),
            pltpu.VMEM((128, 4 * QUARTER), BF),
            pltpu.VMEM((3, QUARTER, 2 * HID), BF),
            pltpu.VMEM((4, SLOTS, WIDE), BF),
            pltpu.VMEM((4, SLOTS, QUARTER), BF),
            pltpu.VMEM((4, SLOTS, WIDE), BF),
            pltpu.VMEM((4, SLOTS, QUARTER), BF),
            pltpu.VMEM((4, 4, 2, SHARD, WIDE), BF),
            pltpu.VMEM((4, 4, 2, SHARD, QUARTER), BF),
            pltpu.VMEM((4, 2, 3, 32, 256), F32),
            pltpu.VMEM((4, 3, 32, 256), F32),
            pltpu.VMEM((4, 3, 32, 256), F32),
            pltpu.VMEM((4, 6, 3, 32, 256), F32),
            pltpu.VMEM((4, 6, 3, 32, 256), F32),
            pltpu.VMEM((4, 4, 2, 3, 32, 256), BF),
            pltpu.VMEM((4, 64, EXTRA), F32),
            pltpu.VMEM((3, 1024, 256), BF),
            pltpu.VMEM((4, 2, SHARD, WIDE), F32),
            pltpu.VMEM((4, SHARD, WIDE), F32),
            pltpu.VMEM((4, SHARD, WIDE), F32),
            pltpu.VMEM((4, 6, SHARD, WIDE), BF),
            pltpu.VMEM((4, 6, SHARD, WIDE), BF),
            pltpu.VMEM((2, SHARD, WIDE), F32),
            pltpu.VMEM((SHARD, WIDE), F32),
            pltpu.VMEM((SHARD, WIDE), F32),
            pltpu.VMEM((6, SHARD, WIDE), BF),
            pltpu.VMEM((6, SHARD, WIDE), BF),
            pltpu.VMEM((SHARD, WIDE), BF),
            pltpu.VMEM((SHARD, WIDE), BF),
            pltpu.VMEM((4, SLOTS, QUARTER), BF),
            pltpu.VMEM((4, SLOTS, QUARTER), BF),
            pltpu.VMEM((3, QUARTER, HID), F32),
            pltpu.SemaphoreType.DMA((UNITS,)),
            pltpu.SemaphoreType.DMA((UNITS,)),
            pltpu.SemaphoreType.DMA((8,)),
        ],
        compiler_params=pltpu.CompilerParams(
            collective_id=0, has_side_effects=True, vmem_limit_bytes=60 * 1024 * 1024
        ),
    )(slot_token, router_weight[None, :], layer_input, out_grad, gate_weight, up_weight, down_weight)

    slots = jnp.arange(SLOTS, dtype=jnp.int32)
    hit = token_slot[:, None] == slots[None, :]
    flat = rows.transpose(1, 0, 2).reshape(SLOTS, 4 * QUARTER)
    input_grad = jnp.dot(hit.astype(BF), flat, preferred_element_type=F32).astype(BF)
    router_grad = jnp.sum(jnp.where(hit, router[None, :, 0], 0.0), axis=1)
    return (input_grad, router_grad, own_gate + peer[0], own_up + peer[1], own_down + peer[2])


def solution(mesh):
    both = ("dp", "ckpt")
    return jax.shard_map(
        local_step,
        mesh=mesh,
        in_specs=(
            P(both, None),
            P(both, None),
            P(both),
            P(both),
            P(both),
            P("ckpt", "dp"),
            P("ckpt", "dp"),
            P("ckpt", "dp"),
        ),
        out_specs=(P(both, None), P(both), P("ckpt", "dp"), P("ckpt", "dp"), P("ckpt", "dp")),
        check_vma=False,
    )
```

time: 765 us -> 155 us (0.20)
  waiting for transfers between devices: 356 us -> 0 us
  blocking collectives: 319 us -> 0 us
  Pallas kernels: 0 us -> 145 us
  matrix products: 36.8 us -> 1.76 us
  between operations: 15.2 us -> 0.66 us
  starting transfers between devices: 12.7 us -> 0 us
  other arithmetic: 12.8 us -> 4.43 us
    unnamed x2 -> x0, blocking collectives: 290 us -> none
    all_gather x2 -> x0, waiting for transfers between devices: 198 us -> none  [the longest x1 102 us: local(): lax.all_gather(quarter_grad, 'dp', axis=0, tiled=True)]
    reduce_scatter x1 -> x0, waiting for transfers between devices: 149 us -> none  [local(): lax.psum_scatter(input_part, 'dp', scatter_dimension=0, tiled=True)]
    pallas_call x0 -> x1, Pallas kernels: none -> 145 us  [local_step(): pl.pallas_call(kernel, out_shape=(jax.ShapeDtypeStruct((4, SLOTS, QUARTER...]
    dot_general x8 -> x1, matrix products: 36.8 us -> 1.76 us  [local_step(): jnp.dot(hit.astype(BF), flat, preferred_element_type=F32).astype(BF)]
    all_to_all x2 -> x0, blocking collectives: 28.2 us -> none  [the longest x1 17 us: local(): lax.all_to_all(rows_input, 'ckpt', split_axis=1, concat_axis=0, tiled=True)]
    all_to_all x2 -> x0, starting transfers between devices: 12.6 us -> none  [the longest x1 6.45 us: local(): lax.all_to_all(router_tile, 'ckpt', split_axis=1, concat_axis=0, tiled=True)]
    all_to_all x2 -> x0, waiting for transfers between devices: 9.38 us -> none  [the longest x1 6.48 us: local(): lax.all_to_all(router_tile, 'ckpt', split_axis=1, concat_axis=0, tiled=True)]
  transfers between devices with their start and end apart: 6 -> 0, of which waited for: 5 -> 0; matrix products, arithmetic and copies ran while one was open for 4% -> 0% of each run, Pallas kernels for 0% -> 0%
where the time goes in v1:
time: 155 us; the launch traced here: 152 us
  Pallas kernels  145 us (94%)
  other arithmetic  4.43 us (3%)
  matrix products  1.76 us (1%)
    pallas_call x1, Pallas kernels, local_step(): pl.pallas_call(kernel, out_shape=(jax.ShapeDtypeStruct((4, SLOTS, QUARTER...  145 us
    add x1, other arithmetic, local_step(): own_down + peer[2]  3.83 us

profile of v1, /device:TPU:2, one launch (start us, length us, event | category | flops | bytes accessed | tf_op | source)
XLA Modules:
  0.0 152.1 jit_solution(9640422746222380262)
XLA Ops:
  0.6 145.1 %shard_map.119 = (bf16[4,8,1536]{2,1,0:T(8,128)(2,1)}, f32[8,128]{1,0:T(8,128)}, f32[1536,128]{1,0:T(8,128)}, f32[1536,128]{1,0:T(8,128)}, f32[1536,128]{1,0:T(8,128)}, /*index=5*/f32[3,1536,128]{2,1,0:T(8,128)}) custom-call(s32[8]{0:T(128)} %slot_ref.1, bf16[1,128]{1,0:T(2,128)(2,1)} %bitcast.12, bf16[128,6144]{1,0:T(8,128)(2,1)} %x_hbm.1, ...), custom_call_target="tpu_custom_call" | custom-call | tf_op jit(solution)/shard_map/pallas_call | solution.py:511
  145.7 0.0 copy-start
  145.7 0.0 copy-start.2
  145.7 3.8 %bitcast_add_fusion = (f32[1536,128]{1,0:T(8,128)}, f32[1536,128]{1,0:T(8,128)}, f32[1536,128]{1,0:T(8,128)}) fusion(f32[1536,128]{1,0:T(8,128)} %get-tuple-element.16, f32[3,1536,128]{2,1,0:T(8,128)} %get-tuple-element.14, f32[1536,128]{1,0:T(8,128)} %get-tuple-element.15, f32[1536,128]{1,0:T(8,128)} %get-tuple-element.13), kind=kLoop, calls=%fused_computation.1 | loop fusion | flops 589824 | bytes 7077888 | tf_op jit(solution)/shard_map/add | solution.py:570
  149.6 0.0 copy-start.1
  149.6 0.0 copy-done
  149.6 0.0 copy-done.2
  149.6 1.8 %convolution_convert_fusion = bf16[128,6144]{1,0:T(8,128)(2,1)} fusion(bf16[8,6144]{1,0:T(8,128)(2,1)S(1)} %bitcast.11, s32[128]{0:T(128)S(1)} %copy-done.2), kind=kOutput, calls=%fused_computation | convolution fusion | flops 13370368 | bytes 1671680 | tf_op jit(solution)/shard_map/dot_general | solution.py:568
  151.3 0.0 copy-done.1
  151.3 0.1 slice_reduce_fusion
  151.5 0.6 select_reduce_fusion
Async XLA Ops:
  145.7 3.9 %copy-start = (bf16[4,8,1536]{2,1,0:T(8,128)(2,1)S(1)}, bf16[4,8,1536]{2,1,0:T(8,128)(2,1)}, u32[]{:S(2)}) copy-start(bf16[4,8,1536]{2,1,0:T(8,128)(2,1)} %get-tuple-element.11) | copy-start | bytes 294916
  145.7 3.9 %copy-start.2 = (s32[128]{0:T(128)S(1)}, s32[128]{0:T(128)}, u32[]{:S(2)}) copy-start(s32[128]{0:T(128)} %param.11) | copy-start | bytes 1540
  149.6 1.8 %copy-start.1 = (f32[8,128]{1,0:T(8,128)S(1)}, f32[8,128]{1,0:T(8,128)}, u32[]{:S(2)}) copy-start(f32[8,128]{1,0:T(8,128)} %get-tuple-element.12) | copy-start | bytes 12292

commit v2 on v1

--- a/solution.py
+++ b/solution.py
@@ -10,6 +10,8 @@
 MESH = pl.DeviceIdType.MESH
 BF = jnp.bfloat16
 F32 = jnp.float32
+I32 = jnp.int32
+I16 = jnp.int16
 
 RIGHT, LEFT, OPP = 1, 2, 3
 OFFSET = (0, 1, 3, 2)
@@ -21,22 +23,24 @@
 SLOTS = 8
 SHARD = 32
 UNITS = 160
+CODED = 112
+STEPS = 32000.0
 
 
 def kernel(
     slot_ref,
     router_ref,
+    token_ref,
     x_hbm,
     g_hbm,
     wg_hbm,
     wu_hbm,
     wd_hbm,
-    rows_out,
+    input_out,
     router_out,
-    own_gate,
-    own_up,
-    own_down,
-    peer_part,
+    gate_out,
+    up_out,
+    down_out,
     xbuf,
     gbuf,
     wcat,
@@ -69,6 +73,8 @@
     last_send,
     last_recv,
     part_send,
+    own_part,
+    peer_part,
     send_sem,
     recv_sem,
     local_sem,
@@ -251,7 +257,35 @@
     reduce_a = [Reduce(lambda u, k=k: es.at[k, u], lambda u, k=k: er.at[k, u], a_right, a_left) for k in range(4)]
     reduce_b = Reduce(lambda u: fs.at[u], lambda u: fr.at[u], b_right, b_left)
 
+    def encode(ref, j, v):
+        exps = []
+        for n in range(4):
+            rows = v[8 * n : 8 * n + 8]
+            top = jnp.max(jnp.abs(rows), axis=0, keepdims=True)
+            exps.append(jnp.ceil(jnp.log2(jnp.maximum(top, 1e-30))))
+        ups = [jnp.exp2(-e) * STEPS for e in exps]
+        scaled = jnp.concatenate([v[8 * n : 8 * n + 8] * ups[n] for n in range(4)], axis=0)
+        ref[pl.ds(32 * j, 32)] = jnp.floor(scaled + 0.5).astype(I32).astype(I16)
+        return exps
+
+    def put_exps(ref, exps):
+        rows = jnp.concatenate(exps + [jnp.zeros((4, 256), F32)], axis=0)
+        ref[pl.ds(96, 16)] = rows.astype(I32).astype(I16)
+
+    def decode(ref):
+        steps = jnp.exp2(ref[pl.ds(96, 16)].astype(I32).astype(F32)) * (1.0 / STEPS)
+        v = ref[pl.ds(0, 96)].astype(I32).astype(F32)
+        out = []
+        for j in range(3):
+            out.append(
+                jnp.concatenate(
+                    [v[8 * n : 8 * n + 8] * steps[n : n + 1] for n in range(4 * j, 4 * j + 4)], axis=0
+                )
+            )
+        return out
+
     def forward(k):
+        exps = [[], [], [], []]
         lhs_x = xa[k, :, :, :, 0:QUARTER].reshape(256, QUARTER)
         lhs_g = ga[k].reshape(256, QUARTER)
         for j, lhs in enumerate((lhs_x, lhs_x, lhs_g)):
@@ -263,20 +297,23 @@
                 ]
                 for p in range(4)
             ]
-            zs[k, 0, j] = piece[OPP][0]
-            zs[k, 1, j] = piece[OPP][1]
-            zs[k, 2, j] = piece[RIGHT][1]
-            zs[k, 3, j] = piece[LEFT][0]
+            for u, v in enumerate((piece[OPP][0], piece[OPP][1], piece[RIGHT][1], piece[LEFT][0])):
+                exps[u] += encode(zs.at[k, u], j, v)
             pre_own[k, 0, j] = piece[0][0]
             pre_own[k, 1, j] = piece[0][1]
             pre_right[k, j] = piece[RIGHT][0]
             pre_left[k, j] = piece[LEFT][1]
+        for u in range(4):
+            put_exps(zs.at[k, u], exps[u])
         reduce_z[k].start()
 
     def relay_z(k):
         def add(side):
             mine = pre_left if side else pre_right
-            zs[k, 4 + side] = mine[k] + zr[k, side]
+            exps = []
+            for j, v in enumerate(decode(zr.at[k, side])):
+                exps += encode(zs.at[k, 4 + side], j, mine[k, j] + v)
+            put_exps(zs.at[k, 4 + side], exps)
 
         reduce_z[k].relay(add)
 
@@ -284,8 +321,8 @@
         reduce_z[k].finish()
         for h in range(2):
             near, far = (2, 5) if h else (3, 4)
-            total = pre_own[k, h] + zr[k, near] + zr[k, far]
-            gate_pre, up_pre, act_grad = total[0], total[1], total[2]
+            first, second = decode(zr.at[k, near]), decode(zr.at[k, far])
+            gate_pre, up_pre, act_grad = [pre_own[k, h, j] + first[j] + second[j] for j in range(3)]
             router = xa[k, 2 * h : 2 * h + 2, :, 0:16, QUARTER:WIDE].astype(F32)[:, :, 0:8].reshape(32, EXTRA)
             router = jnp.concatenate([router, router], axis=1)
             sigmoid_g = jax.nn.sigmoid(gate_pre)
@@ -402,9 +439,9 @@
         tn = (((0,), (0,)), ((), ()))
         lhs_x = xa[:, :, :, :, cols].reshape(1024, 256)
         lhs_g = ga[:, :, :, :, cols].reshape(1024, 256)
-        for j, (lhs, own) in enumerate(((lhs_x, own_gate), (lhs_x, own_up), (lhs_g, own_down))):
+        for j, lhs in enumerate((lhs_x, lhs_x, lhs_g)):
             dw = lax.dot_general(lhs, dmat[j], tn, preferred_element_type=F32)
-            own[cols, :] = dw[:, 0:HID]
+            own_part[j, cols, :] = dw[:, 0:HID]
             part_send[j, cols, :] = dw[:, HID:]
         return carry
 
@@ -480,17 +517,32 @@
     swap.wait_recv()
     total = f_own[0] + zl_recv[...].astype(F32)
     router_sum = total[0:8, QUARTER:WIDE] + total[8:16, QUARTER:WIDE]
-    router_out[...] = jnp.broadcast_to(jnp.sum(router_sum, axis=1, keepdims=True), (SLOTS, EXTRA))
     for p in range(4):
         last_send[p] = total[8 * p : 8 * p + 8, 0:QUARTER].astype(BF)
     last = [send(last_send.at[p], last_recv.at[MIRROR[p]], z_at[p]) for p in (3, 1, 2)]
-    rows_out[m] = last_send[0]
-    for p, copy in zip((3, 1, 2), last):
+
+    hit = lax.broadcasted_iota(jnp.int32, (SLOTS, 128), 0) == token_ref[...]
+    router_rows = jnp.sum(router_sum, axis=1, keepdims=True)
+    router_out[...] = jnp.sum(jnp.where(hit, router_rows, 0.0), axis=0, keepdims=True)
+    hot = jnp.concatenate([jnp.where(hit, 1.0, 0.0), jnp.zeros((SLOTS, 128), F32)], axis=0).astype(BF)
+    stores = []
+
+    def place(p, rows):
+        rows = jnp.concatenate([rows.astype(F32), jnp.zeros((SLOTS, QUARTER), F32)], axis=0).astype(BF)
+        spread = lax.dot_general(hot, rows, (((0,), (0,)), ((), ())), preferred_element_type=F32)
+        xbuf[:, quarters[p]] = spread.astype(BF)
+
+    place(0, last_send[0])
+    for j, out in enumerate((gate_out, up_out, down_out)):
+        part[j].wait_recv()
+        own_part[j] = own_part[j] + peer_part[j]
+        stores.append(local(own_part.at[j], out))
+    for p, copy in zip((2, 1, 3), (last[1], last[2], last[0])):
         copy.wait_recv()
-    for p in (1, 2, 3):
-        rows_out[lax.rem(m + OFFSET[p], 4)] = last_recv[p]
-    for copy in part:
-        copy.wait_recv()
+        place(p, last_recv[p])
+    stores.append(local(xbuf, input_out))
+    for copy in stores:
+        copy.wait()
     for copy in sent:
         copy.wait_send()
 
@@ -508,18 +560,17 @@
     any_ = pl.BlockSpec(memory_space=pl.ANY)
     vmem = pl.BlockSpec(memory_space=pltpu.VMEM)
     grad = jax.ShapeDtypeStruct((QUARTER, HID), F32)
-    rows, router, own_gate, own_up, own_down, peer = pl.pallas_call(
+    input_grad, router, gate_grad, up_grad, down_grad = pl.pallas_call(
         kernel,
         out_shape=(
-            jax.ShapeDtypeStruct((4, SLOTS, QUARTER), BF),
-            jax.ShapeDtypeStruct((SLOTS, EXTRA), F32),
+            jax.ShapeDtypeStruct((128, 4 * QUARTER), BF),
+            jax.ShapeDtypeStruct((1, 128), F32),
             grad,
             grad,
             grad,
-            jax.ShapeDtypeStruct((3, QUARTER, HID), F32),
         ),
-        in_specs=[pl.BlockSpec(memory_space=pltpu.SMEM), vmem, any_, any_, any_, any_, any_],
-        out_specs=(vmem, vmem, vmem, vmem, vmem, any_),
+        in_specs=[pl.BlockSpec(memory_space=pltpu.SMEM), vmem, vmem, any_, any_, any_, any_, any_],
+        out_specs=(any_, vmem, any_, any_, any_),
         scratch_shapes=[
             pltpu.VMEM((128, 4 * QUARTER), BF),
             pltpu.VMEM((128, 4 * QUARTER), BF),
@@ -533,8 +584,8 @@
             pltpu.VMEM((4, 2, 3, 32, 256), F32),
             pltpu.VMEM((4, 3, 32, 256), F32),
             pltpu.VMEM((4, 3, 32, 256), F32),
-            pltpu.VMEM((4, 6, 3, 32, 256), F32),
-            pltpu.VMEM((4, 6, 3, 32, 256), F32),
+            pltpu.VMEM((4, 6, CODED, 256), I16),
+            pltpu.VMEM((4, 6, CODED, 256), I16),
             pltpu.VMEM((4, 4, 2, 3, 32, 256), BF),
             pltpu.VMEM((4, 64, EXTRA), F32),
             pltpu.VMEM((3, 1024, 256), BF),
@@ -553,21 +604,26 @@
             pltpu.VMEM((4, SLOTS, QUARTER), BF),
             pltpu.VMEM((4, SLOTS, QUARTER), BF),
             pltpu.VMEM((3, QUARTER, HID), F32),
+            pltpu.VMEM((3, QUARTER, HID), F32),
+            pltpu.VMEM((3, QUARTER, HID), F32),
             pltpu.SemaphoreType.DMA((UNITS,)),
             pltpu.SemaphoreType.DMA((UNITS,)),
-            pltpu.SemaphoreType.DMA((8,)),
+            pltpu.SemaphoreType.DMA((16,)),
         ],
         compiler_params=pltpu.CompilerParams(
             collective_id=0, has_side_effects=True, vmem_limit_bytes=60 * 1024 * 1024
         ),
-    )(slot_token, router_weight[None, :], layer_input, out_grad, gate_weight, up_weight, down_weight)
-
-    slots = jnp.arange(SLOTS, dtype=jnp.int32)
-    hit = token_slot[:, None] == slots[None, :]
-    flat = rows.transpose(1, 0, 2).reshape(SLOTS, 4 * QUARTER)
-    input_grad = jnp.dot(hit.astype(BF), flat, preferred_element_type=F32).astype(BF)
-    router_grad = jnp.sum(jnp.where(hit, router[None, :, 0], 0.0), axis=1)
-    return (input_grad, router_grad, own_gate + peer[0], own_up + peer[1], own_down + peer[2])
+    )(
+        slot_token,
+        router_weight[None, :],
+        token_slot[None, :],
+        layer_input,
+        out_grad,
+        gate_weight,
+        up_weight,
+        down_weight,
+    )
+    return (input_grad, router[0], gate_grad, up_grad, down_grad)
 
 
 def solution(mesh):

time: 155 us -> 136 us (0.88); the launches traced: 152 us -> 136 us
  Pallas kernels: 145 us -> 130 us
  local copies, waits for them, and re-layouts: 0.13 us -> 5.93 us
  other arithmetic: 4.43 us -> 0 us
  matrix products: 1.76 us -> 0 us
    pallas_call x1, Pallas kernels: 145 us -> 130 us  [local_step(): pl.pallas_call(kernel, out_shape=(jax.ShapeDtypeStruct((128, 4 * QUARTER)...]
    unnamed x6 -> x13, local copies, waits for them, and re-layouts: 0.01 us -> 5.93 us
    add x1 -> x0, other arithmetic: 3.83 us -> none  [local_step(): own_down + peer[2]]
    dot_general x1 -> x0, matrix products: 1.76 us -> none  [local_step(): jnp.dot(hit.astype(BF), flat, preferred_element_type=F32).astype(BF)]
where the time goes in v2:
time: 136 us
  Pallas kernels  130 us (96%)
  local copies, waits for them, and re-layouts  5.93 us (4%)
    pallas_call x1, Pallas kernels, local_step(): pl.pallas_call(kernel, out_shape=(jax.ShapeDtypeStruct((128, 4 * QUARTER)...  130 us
    unnamed x13, local copies, waits for them, and re-layouts  5.93 us

profile of v2, /device:TPU:2, one launch (start us, length us, event | category | flops | bytes accessed | tf_op | source)
XLA Modules:
  0.0 136.2 jit_solution(7061917790742927154)
XLA Ops:
  0.6 129.6 %shard_map.119 = (bf16[128,6144]{1,0:T(8,128)(2,1)}, f32[1,128]{1,0:T(1,128)}, f32[1536,128]{1,0:T(8,128)}, f32[1536,128]{1,0:T(8,128)}, f32[1536,128]{1,0:T(8,128)}) custom-call(s32[8]{0:T(128)} %slot_ref.1, bf16[1,128]{1,0:T(2,128)(2,1)} %bitcast.3, s32[1,128]{1,0:T(1,128)} %bitcast.4, bf16[128,6144]{1,0:T(8,128)(2,1)} %x_hbm.1, bf16[128,6144]{1,0:T(8,128)(2,1)} %g_hbm.1, ...), custom_call_target="tpu_custom_call" | custom-call | tf_op jit(solution)/shard_map/pallas_call | solution.py:563
  130.3 0.0 copy-start.3
  130.3 0.0 copy-start.2
  130.3 2.8 %copy.18 = bf16[128,6144]{1,0:T(8,128)(2,1)} copy(bf16[128,6144]{1,0:T(8,128)(2,1)} %get-tuple-element.20) | data formatting | bytes 3145728
  133.1 0.0 copy-done.3
  133.1 0.0 copy-start.1
  133.1 0.5 copy.19
  133.6 0.0 copy-done.2
  133.6 0.0 copy-start
  133.6 0.9 copy.20
  134.5 0.0 copy-done.1
  134.5 0.9 copy.21
  135.4 0.0 copy-done
  135.4 0.9 copy.22
Async XLA Ops:
  130.3 2.8 %copy-start.3 = (f32[1,128]{1,0:T(1,128)S(1)}, f32[1,128]{1,0:T(1,128)}, u32[]{:S(2)}) copy-start(f32[1,128]{1,0:T(1,128)} %get-tuple-element.11) | copy-start | bytes 1540
  130.3 3.3 %copy-start.2 = (f32[1536,128]{1,0:T(8,128)S(1)}, f32[1536,128]{1,0:T(8,128)}, u32[]{:S(2)}) copy-start(f32[1536,128]{1,0:T(8,128)} %get-tuple-element.22) | copy-start | bytes 2359300
  133.1 1.4 %copy-start.1 = (f32[1536,128]{1,0:T(8,128)S(1)}, f32[1536,128]{1,0:T(8,128)}, u32[]{:S(2)}) copy-start(f32[1536,128]{1,0:T(8,128)} %get-tuple-element.23) | copy-start | bytes 2359300
  133.6 1.8 %copy-start = (f32[1536,128]{1,0:T(8,128)S(1)}, f32[1536,128]{1,0:T(8,128)}, u32[]{:S(2)}) copy-start(f32[1536,128]{1,0:T(8,128)} %get-tuple-element.24) | copy-start | bytes 2359300
